TPU v7x, 32 devices: a whole 2x2x4 slice. The times are simulated.
32 devices in a mesh: dp: 8 (over z, y), expert: 4 (over x, core).
Axes of the slice: x: 2, y: 2, z: 4, core: 2. Of those that a mesh axis runs over, the one named last changes fastest.
Arguments:
- tokens: bfloat16 [4096, 2048], P(('dp', 'expert')), may hold values from -6 to 6
- routes: int32 [4096, 8], P(('dp', 'expert')), may hold values from 0 to 15, all different within a row; in each aligned block of 128 rows (0 to 127, 128 to 255, ...) at most 80 rows name the same one
- gates: bfloat16 [4096, 8], P(('dp', 'expert')), may hold values from 0.099609375 to 0.5
- cotangent: bfloat16 [4096, 2048], P(('dp', 'expert')), may hold values from -6 to 6
- w_gate: bfloat16 [16, 2048, 384], P('dp'), may hold values from -0.125 to 0.125
- w_up: bfloat16 [16, 2048, 384], P('dp'), may hold values from -0.125 to 0.125
- w_down: bfloat16 [16, 384, 2048], P('dp'), may hold values from -0.3125 to 0.3125
Outputs:
- layer_out: bfloat16 [4096, 2048], P(('dp', 'expert'))
- grad_tokens: bfloat16 [4096, 2048], P(('dp', 'expert'))
- grad_gate: bfloat16 [16, 2048, 384], P('dp', 'expert')
- grad_up: bfloat16 [16, 2048, 384], P('dp', 'expert')
- grad_down: bfloat16 [16, 384, 2048], P('dp', None, 'expert')
Inputs may be any that keep to these rules, and one draw needn't show every extreme that they name: `routes`: each row names 8 different experts. Among the rows of one device, no expert is named by more than 80 rows, and in every draw some device has an expert named by exactly 80 rows.
All inputs are finite; a program needn't handle non-finite values.
Results may differ from a plain program's by a relative error of at most 0.012.
Values may be sent and summed in bfloat16 or wider, within the bound.
A program may use at most 128 MiB of HBM per device.

v0:
```python
import jax
import jax.numpy as jnp
from jax import lax
from jax.sharding import PartitionSpec as P


def expert_forward(arrived, w_gate, w_up, w_down):
    gate_act = jnp.einsum("erd,edf->erf", arrived, w_gate, preferred_element_type=jnp.float32)
    up_act = jnp.einsum("erd,edf->erf", arrived, w_up, preferred_element_type=jnp.float32)
    sigma_gate = jax.nn.sigmoid(gate_act)
    smooth = gate_act * sigma_gate
    hidden = (smooth * up_act).astype(jnp.bfloat16)
    result = jnp.einsum("erf,efd->erd", hidden, w_down, preferred_element_type=jnp.float32).astype(
        jnp.bfloat16
    )
    return (gate_act, up_act, sigma_gate, smooth, hidden, result)


def body(tokens, routes, gates, cotangent, w_gate, w_up, w_down):
    tok_rows, top_k = routes.shape
    width = tokens.shape[1]
    owners = lax.axis_size("dp")
    per_owner = w_gate.shape[0]
    hidden_units = w_gate.shape[2]
    experts = owners * per_owner
    capacity = max(2, tok_rows * top_k * 5 // (4 * experts))
    slot_count = experts * capacity
    chosen = routes.reshape(-1)
    onehot = (chosen[:, None] == jnp.arange(experts, dtype=jnp.int32)[None, :]).astype(jnp.int32)
    order_in = jnp.sum((jnp.cumsum(onehot, axis=0) - onehot) * onehot, axis=1)
    slot_index = chosen * capacity + order_in
    token_of = jnp.arange(tok_rows * top_k, dtype=jnp.int32) // top_k
    table = jnp.full((slot_count,), tok_rows, jnp.int32).at[slot_index].set(token_of)
    slot_gain = (
        jnp.zeros((slot_count,), jnp.float32)
        .at[slot_index]
        .set(gates.reshape(-1).astype(jnp.float32))
    )
    padded_x = jnp.concatenate([tokens, jnp.zeros((1, width), tokens.dtype)], axis=0)
    padded_c = jnp.concatenate([cotangent, jnp.zeros((1, width), cotangent.dtype)], axis=0)
    send_rows = padded_x[table].reshape(experts, capacity, width)
    send_grads = (slot_gain[:, None] * padded_c[table].astype(jnp.float32)).astype(jnp.bfloat16)
    send_grads = send_grads.reshape(experts, capacity, width)
    arrived = lax.all_to_all(send_rows, "dp", split_axis=0, concat_axis=1, tiled=True)
    state = expert_forward(arrived, w_gate, w_up, w_down)
    arrived_grad = lax.all_to_all(send_grads, "dp", split_axis=0, concat_axis=1, tiled=True)
    gate_act, up_act, sigma_gate, smooth, hidden, result = state
    returned = lax.all_to_all(result, "dp", split_axis=1, concat_axis=0, tiled=True).reshape(
        slot_count, width
    )
    picked = returned[slot_index].reshape(tok_rows, top_k, width)
    layer_out = jnp.einsum("tk,tkd->td", gates, picked, preferred_element_type=jnp.float32).astype(
        jnp.bfloat16
    )
    grad_hidden = jnp.einsum(
        "erd,efd->erf", arrived_grad, w_down, preferred_element_type=jnp.float32
    )
    grad_upact = (grad_hidden * smooth).astype(jnp.bfloat16)
    grad_gateact = (
        grad_hidden * up_act * sigma_gate * (1.0 + gate_act * (1.0 - sigma_gate))
    ).astype(jnp.bfloat16)
    row_grads = (
        jnp.einsum("erf,edf->erd", grad_gateact, w_gate, preferred_element_type=jnp.float32)
        + jnp.einsum("erf,edf->erd", grad_upact, w_up, preferred_element_type=jnp.float32)
    ).astype(jnp.bfloat16)
    came_back = lax.all_to_all(row_grads, "dp", split_axis=1, concat_axis=0, tiled=True).reshape(
        slot_count, width
    )
    grad_picked = came_back[slot_index].reshape(tok_rows, top_k, width)
    grad_tokens = jnp.sum(grad_picked.astype(jnp.float32), axis=1).astype(jnp.bfloat16)
    both_factors = jnp.concatenate([grad_gateact, grad_upact], axis=2)
    input_term = jnp.einsum(
        "erd,erf->def", arrived, both_factors, preferred_element_type=jnp.float32
    )
    down_term = jnp.einsum("erf,erd->def", hidden, arrived_grad, preferred_element_type=jnp.float32)
    totals = lax.psum_scatter(
        jnp.concatenate([input_term, down_term], axis=2).astype(jnp.bfloat16),
        "expert",
        scatter_dimension=0,
        tiled=True,
    ).astype(jnp.float32)
    grad_gate = jnp.transpose(totals[:, :, :hidden_units], (1, 0, 2)).astype(jnp.bfloat16)
    grad_up = jnp.transpose(totals[:, :, hidden_units : 2 * hidden_units], (1, 0, 2)).astype(
        jnp.bfloat16
    )
    grad_down = jnp.transpose(totals[:, :, 2 * hidden_units :], (1, 2, 0)).astype(jnp.bfloat16)
    return (layer_out, grad_tokens, grad_gate, grad_up, grad_down)


def solution(mesh):
    return jax.shard_map(
        body,
        mesh=mesh,
        in_specs=(
            P(("dp", "expert"), None),
            P(("dp", "expert"), None),
            P(("dp", "expert"), None),
            P(("dp", "expert"), None),
            P("dp", None, None),
            P("dp", None, None),
            P("dp", None, None),
        ),
        out_specs=(
            P(("dp", "expert"), None),
            P(("dp", "expert"), None),
            P("dp", "expert", None),
            P("dp", "expert", None),
            P("dp", None, "expert"),
        ),
        check_vma=False,
    )
```

profile of v0, /device:TPU:0, one launch (start us, length us, event | category | flops | bytes accessed | tf_op | source)
XLA Modules:
  0.0 627.4 jit_solution(449941669003016595)
XLA Ops:
  9.0 4.5 reduce-window.6
  25.7 11.9 %gather_fusion.2 = bf16[1280,2048]{1,0:T(8,128)(2,1)} fusion(bf16[129,2048]{1,0:T(8,128)(2,1)} %concatenate.14, s32[2048]{0:T(1024)S(1)} %pad_clamp_fusion), kind=kCustom, calls=%fused_computation.2 | custom fusion | bytes 10490880 | tf_op jit(solution)/shard_map/gather | solution.py:42
  37.7 5.7 fusion
  43.4 7.3 %all-to-all-start.2 = ((bf16[16,80,2048]{2,1,0:T(8,128)(2,1)}), bf16[16,80,2048]{2,1,0:T(8,128)(2,1)}, u32[]{:S(2)}, u32[]{:S(2)}) async-start(bf16[16,80,2048]{2,1,0:T(8,128)(2,1)} %fusion), calls=%async_computation.2 | async-start | bytes 10485760 | tf_op jit(solution)/shard_map/all_to_all | solution.py:46
  52.6 12.0 %gather_fusion = bf16[1280,2048]{1,0:T(8,128)(2,1)} fusion(bf16[129,2048]{1,0:T(8,128)(2,1)} %concatenate.13, s32[2048]{0:T(1024)S(1)} %pad_clamp_fusion), kind=kCustom, calls=%fused_computation | custom fusion | bytes 10490880 | tf_op jit(solution)/shard_map/gather | solution.py:41
  64.5 101.9 %all-to-all-done.2 = bf16[16,80,2048]{2,1,0:T(8,128)(2,1)} async-done(((bf16[16,80,2048]{2,1,0:T(8,128)(2,1)}), bf16[16,80,2048]{2,1,0:T(8,128)(2,1)}, u32[]{:S(2)}, u32[]{:S(2)}) %all-to-all-start.2) | async-done | bytes 5242912 | tf_op jit(solution)/shard_map/all_to_all | solution.py:46
  166.4 4.8 all-to-all-start
  171.3 5.6 copy.52
  176.9 109.3 %all-to-all-done = bf16[16,80,2048]{2,1,0:T(8,128)(2,1)} async-done(((bf16[16,80,2048]{2,1,0:T(8,128)(2,1)}), bf16[16,80,2048]{2,1,0:T(8,128)(2,1)}, u32[]{:S(2)}, u32[]{:S(2)}) %all-to-all-start) | async-done | bytes 5242912 | tf_op jit(solution)/shard_map/all_to_all | solution.py:44
  297.9 6.0 multiply_convert_fusion
  307.1 7.1 %convert_bitcast_fusion = bf16[2048,2,768]{0,2,1:T(8,128)(2,1)} fusion(bf16[2,640,2048]{2,1,0:T(8,128)(2,1)S(1)} %bitcast.86, bf16[2,640,384]{1,2,0:T(8,128)(2,1)S(1)} %copy-done.7, bf16[2,640,384]{1,2,0:T(8,128)(2,1)S(1)} %get-tuple-element.21), kind=kOutput, calls=%fused_computation.10 | convolution fusion | flops 4033609728 | bytes 13500416 | tf_op jit(solution)/shard_map/erd,erf->def/dot_general | solution.py:72
  318.2 5.2 add_convert_fusion
  323.4 10.2 %copy.55 = bf16[2,640,2048]{2,0,1:T(2,128)(2,1)} copy(bf16[2,640,2048]{2,1,0:T(8,128)(2,1)} %add_convert_fusion) | data formatting | bytes 10485760 | tf_op jit(solution)/shard_map/convert_element_type | solution.py:65
  333.6 4.7 all-to-all-start.3
  338.4 8.2 %pad_maximum_fusion = bf16[2048,2,1152]{0,2,1:T(8,128)(2,1)} fusion(bf16[2048,2,384]{0,2,1:T(8,128)(2,1)} %fusion.3, bf16[2048,2,768]{0,2,1:T(8,128)(2,1)} %convert_bitcast_fusion), kind=kLoop, calls=%fused_computation.9 | loop fusion | flops 18874368 | bytes 18874368 | tf_op jit(solution)/shard_map/concatenate | solution.py:77
  346.6 5.9 convolution_convert_fusion
  352.6 11.0 %copy.49 = bf16[2,640,2048]{2,0,1:T(2,128)(2,1)} copy(bf16[2,640,2048]{2,1,0:T(8,128)(2,1)} %convolution_convert_fusion) | data formatting | bytes 10485760 | tf_op jit(solution)/shard_map/convert_element_type | solution.py:13
  363.6 89.6 %all-to-all-done.3 = bf16[2,640,2048]{2,0,1:T(2,128)(2,1)} async-done(((bf16[2,640,2048]{2,0,1:T(2,128)(2,1)}), bf16[2,640,2048]{2,0,1:T(2,128)(2,1)}, u32[]{:S(2)}, u32[]{:S(2)}) %all-to-all-start.3) | async-done | bytes 5242912 | tf_op jit(solution)/shard_map/all_to_all | solution.py:66
  453.2 4.8 all-to-all-start.1
  458.2 7.2 %copy.56 = bf16[2,8,80,2048]{3,2,0,1:T(8,128)(2,1)} copy(bf16[2,8,80,2048]{3,0,2,1:T(2,128)(2,1)} %bitcast.18) | data formatting | bytes 10485760 | tf_op jit(solution)/shard_map/all_to_all | solution.py:66
  465.4 107.5 %all-to-all-done.1 = bf16[2,640,2048]{2,0,1:T(2,128)(2,1)} async-done(((bf16[2,640,2048]{2,0,1:T(2,128)(2,1)}), bf16[2,640,2048]{2,0,1:T(2,128)(2,1)}, u32[]{:S(2)}, u32[]{:S(2)}) %all-to-all-start.1) | async-done | bytes 5242912 | tf_op jit(solution)/shard_map/all_to_all | solution.py:48
  572.9 7.3 %copy.50 = bf16[2,8,80,2048]{3,2,0,1:T(8,128)(2,1)} copy(bf16[2,8,80,2048]{3,0,2,1:T(2,128)(2,1)} %bitcast.8) | data formatting | bytes 10485760 | tf_op jit(solution)/shard_map/all_to_all | solution.py:48
  580.2 12.0 %gather_fusion.3 = bf16[1024,2048]{1,0:T(8,128)(2,1)} fusion(bf16[1280,2048]{1,0:T(8,128)(2,1)} %bitcast.74, s32[1024]{0:T(1024)S(1)} %broadcast_clamp_fusion), kind=kCustom, calls=%fused_computation.3 | custom fusion | bytes 8392704 | tf_op jit(solution)/shard_map/gather | solution.py:69
  592.2 12.2 %gather_fusion.1 = bf16[1024,2048]{1,0:T(8,128)(2,1)} fusion(bf16[1280,2048]{1,0:T(8,128)(2,1)} %bitcast.75, s32[1024]{0:T(1024)S(1)} %broadcast_clamp_fusion), kind=kCustom, calls=%fused_computation.1 | custom fusion | bytes 8392704 | tf_op jit(solution)/shard_map/gather | solution.py:51
  (73 shorter events, 50.9 us)
Async XLA Ops:
  7.2 290.7 %copy-start = (bf16[2,384,2048]{2,1,0:T(8,128)(2,1)S(1)}, bf16[2,384,2048]{2,1,0:T(8,128)(2,1)}, u32[]{:S(2)}) copy-start(bf16[2,384,2048]{2,1,0:T(8,128)(2,1)} %param.13) | copy-start | bytes 9437188
  43.4 123.1 %all-to-all-start.2 = ((bf16[16,80,2048]{2,1,0:T(8,128)(2,1)}), bf16[16,80,2048]{2,1,0:T(8,128)(2,1)}, u32[]{:S(2)}, u32[]{:S(2)}) async-start(bf16[16,80,2048]{2,1,0:T(8,128)(2,1)} %fusion), calls=%async_computation.2 | async-start | bytes 10485760 | tf_op jit(solution)/shard_map/all_to_all | solution.py:46
  166.4 119.7 %all-to-all-start = ((bf16[16,80,2048]{2,1,0:T(8,128)(2,1)}), bf16[16,80,2048]{2,1,0:T(8,128)(2,1)}, u32[]{:S(2)}, u32[]{:S(2)}) async-start(bf16[16,80,2048]{2,1,0:T(8,128)(2,1)} %bitcast.76), calls=%async_computation | async-start | bytes 10485760 | tf_op jit(solution)/shard_map/all_to_all | solution.py:44
  286.2 3.4 copy-start.4
  289.3 4.5 copy-start.2
  289.6 4.2 copy-start.5
  289.6 8.3 %slice-start = ((s8[5242880]{0:T(1024)(128)(4,1)}), s8[4194304]{0:T(1024)(128)(4,1)S(1)}, s32[]{:S(2)}) async-start(s8[5242880]{0:T(1024)(128)(4,1)} %bitcast.78), calls=%async_computation.6 | async-start | bytes 8388608
  293.8 4.1 slice-start.1
  303.9 3.2 copy-start.3
  303.9 3.2 copy-start.7
  303.9 10.3 %slice-start.2 = ((s8[5242880]{0:T(1024)(128)(4,1)}), s8[4194304]{0:T(1024)(128)(4,1)S(1)}, s32[]{:S(2)}) async-start(s8[5242880]{0:T(1024)(128)(4,1)} %bitcast.81), calls=%async_computation.8 | async-start | bytes 8388608
  307.1 7.2 %slice-start.3 = ((s8[5242880]{0:T(1024)(128)(4,1)}), s8[1048576]{0:T(1024)(128)(4,1)S(1)}, s32[]{:S(2)}) async-start(s8[5242880]{0:T(1024)(128)(4,1)} %bitcast.81), calls=%async_computation.9 | async-start | bytes 2097152
  307.1 7.1 %copy-start.10 = (bf16[2,640,384]{1,2,0:T(8,128)(2,1)S(1)}, bf16[2,640,384]{1,2,0:T(8,128)(2,1)}, u32[]{:S(2)}) copy-start(bf16[2,640,384]{1,2,0:T(8,128)(2,1)} %get-tuple-element.22) | copy-start | bytes 2949124
  314.2 4.0 copy-start.6
  314.2 4.0 copy-start.8
  333.6 119.6 %all-to-all-start.3 = ((bf16[2,640,2048]{2,0,1:T(2,128)(2,1)}), bf16[2,640,2048]{2,0,1:T(2,128)(2,1)}, u32[]{:S(2)}, u32[]{:S(2)}) async-start(bf16[2,640,2048]{2,0,1:T(2,128)(2,1)} %copy.55), calls=%async_computation.3 | async-start | bytes 10485760 | tf_op jit(solution)/shard_map/all_to_all | solution.py:66
  338.4 274.3 %reduce-scatter.2.cloned.1.call-start = ((), (), s32[]{:S(2)}) async-start(), calls=%async_computation.5 | async-start | bytes 11796480 | tf_op jit(solution)/shard_map/reduce_scatter | solution.py:76
  363.6 94.4 %copy-start.9 = (bf16[128,8]{0,1:T(8,128)(2,1)S(1)}, bf16[128,8]{0,1:T(8,128)(2,1)}, u32[]{:S(2)}) copy-start(bf16[128,8]{0,1:T(8,128)(2,1)} %param.9) | copy-start | bytes 6148
  453.2 119.7 %all-to-all-start.1 = ((bf16[2,640,2048]{2,0,1:T(2,128)(2,1)}), bf16[2,640,2048]{2,0,1:T(2,128)(2,1)}, u32[]{:S(2)}, u32[]{:S(2)}) async-start(bf16[2,640,2048]{2,0,1:T(2,128)(2,1)} %copy.49), calls=%async_computation.1 | async-start | bytes 10485760 | tf_op jit(solution)/shard_map/all_to_all | solution.py:48
  604.3 4.7 copy-start.1
Sparse Core Ops, SparseCore 0:
  346.8 79.0 reduce-scatter.1
where the time goes:
time: 635 us; the launch traced here: 627 us
  waiting for transfers between devices  408 us (64%)
  local copies, waits for them, and re-layouts  117 us (18%)
  matrix products  43.2 us (7%)
  other arithmetic  23 us (4%)
  starting transfers between devices  21.7 us (3%)
  between operations  14.5 us (2%)
    all_to_all x1, waiting for transfers between devices, body(): lax.all_to_all(send_rows, 'dp', split_axis=0, concat_axis=1, tiled=True)  109 us
    all_to_all x1, waiting for transfers between devices, body(): lax.all_to_all(result, 'dp', split_axis=1, concat_axis=0, tiled=True)  108 us
    all_to_all x1, waiting for transfers between devices, body(): lax.all_to_all(send_grads, 'dp', split_axis=0, concat_axis=1, tiled=True)  102 us
    all_to_all x1, waiting for transfers between devices, body(): lax.all_to_all(row_grads, 'dp', split_axis=1, concat_axis=0, tiled=True)  89.6 us
  transfers between devices with their start and end apart: 5, of which 4 were waited for; matrix products, arithmetic and copies ran while one was open for 15% of the time, Pallas kernels for 0%

commit v1 on v0

--- a/solution.py
+++ b/solution.py
@@ -2,6 +2,20 @@
 import jax.numpy as jnp
 from jax import lax
 from jax.sharding import PartitionSpec as P
+
+
+def pools_direct(x0, dim_k, chunk):
+    n_now = x0.shape
+    far_arr = x0.reshape(*n_now[:dim_k], chunk, n_now[dim_k] // chunk, *n_now[dim_k + 1 :])
+    return jnp.moveaxis(far_arr, dim_k, 0)
+
+
+def bind_the_case(mine_x, join_dim):
+    mine_x = jnp.moveaxis(mine_x, 0, join_dim)
+    wide_out = mine_x.shape
+    return mine_x.reshape(
+        *wide_out[:join_dim], wide_out[join_dim] * wide_out[join_dim + 1], *wide_out[join_dim + 2 :]
+    )
 
 
 def expert_forward(arrived, w_gate, w_up, w_down):
@@ -45,9 +59,24 @@
     state = expert_forward(arrived, w_gate, w_up, w_down)
     arrived_grad = lax.all_to_all(send_grads, "dp", split_axis=0, concat_axis=1, tiled=True)
     gate_act, up_act, sigma_gate, smooth, hidden, result = state
-    returned = lax.all_to_all(result, "dp", split_axis=1, concat_axis=0, tiled=True).reshape(
-        slot_count, width
-    )
+
+    def view_surface(sample, axis_tag, u, original):
+        seen_now = lax.axis_size(axis_tag)
+        f_now = lax.axis_index(axis_tag)
+        ready, current_block = (seen_now, f_now)
+        mid_arr = pools_direct(sample, u, ready)
+        buffer = [mid_arr[current_block]]
+        for nth in range(1, ready):
+            response = mid_arr[current_block ^ nth]
+            v_now = lax.ppermute(
+                response, axis_name=axis_tag, perm=[(ii, ii ^ nth) for ii in range(ready)]
+            )
+            buffer.append(v_now)
+        high = jnp.stack(buffer, 0)
+        mid_arr = high[current_block ^ jnp.arange(ready)]
+        return bind_the_case(mid_arr, original)
+
+    returned = view_surface(result, "dp", 1, 0).reshape(slot_count, width)
     picked = returned[slot_index].reshape(tok_rows, top_k, width)
     layer_out = jnp.einsum("tk,tkd->td", gates, picked, preferred_element_type=jnp.float32).astype(
         jnp.bfloat16

time: 635 us -> 647 us (1.019)
  starting transfers between devices: 21.7 us -> 34.4 us
    ppermute x0 -> x7, waiting for transfers between devices: none -> 202 us  [view_surface(): lax.ppermute(response, axis_name=axis_tag, perm=[(ii, ii ^ nth) for ii in...]
    all_to_all x1 -> x0, waiting for transfers between devices: 108 us -> none  [body(): lax.all_to_all(result, 'dp', split_axis=1, concat_axis=0, tiled=True)]
    all_to_all x1, waiting for transfers between devices: 89.6 us -> 0.01 us  [body(): lax.all_to_all(row_grads, 'dp', split_axis=1, concat_axis=0, tiled=True)]
    ppermute x0 -> x7, starting transfers between devices: none -> 16.9 us  [view_surface(): lax.ppermute(response, axis_name=axis_tag, perm=[(ii, ii ^ nth) for ii in...]
    convert_element_type x1 -> x0, local copies, waits for them, and re-layouts: 11 us -> none  [expert_forward(): jnp.einsum('erf,efd->erd', hidden, w_down, preferred_element_type=jnp.flo...]
    all_to_all x1 -> x0, local copies, waits for them, and re-layouts: 7.26 us -> none  [body(): lax.all_to_all(result, 'dp', split_axis=1, concat_axis=0, tiled=True)]
  transfers between devices with their start and end apart: 5 -> 11, of which waited for: 4 -> 6; matrix products, arithmetic and copies ran while one was open for 15% -> 16% of each run, Pallas kernels for 0% -> 0%
where the time goes in v1:
time: 647 us; the launch traced here: 639 us
  waiting for transfers between devices  412 us (64%)
  local copies, waits for them, and re-layouts  113 us (17%)
  matrix products  38.9 us (6%)
  starting transfers between devices  34.4 us (5%)
  other arithmetic  25.8 us (4%)
  between operations  14.9 us (2%)
    ppermute x7, waiting for transfers between devices, view_surface(): lax.ppermute(response, axis_name=axis_tag, perm=[(ii, ii ^ nth) for ii in...  202 us
    all_to_all x1, waiting for transfers between devices, body(): lax.all_to_all(send_rows, 'dp', split_axis=0, concat_axis=1, tiled=True)  109 us
    all_to_all x1, waiting for transfers between devices, body(): lax.all_to_all(send_grads, 'dp', split_axis=0, concat_axis=1, tiled=True)  102 us
    ppermute x7, starting transfers between devices, view_surface(): lax.ppermute(response, axis_name=axis_tag, perm=[(ii, ii ^ nth) for ii in...  16.9 us
  transfers between devices with their start and end apart: 11, of which 6 were waited for; matrix products, arithmetic and copies ran while one was open for 16% of the time, Pallas kernels for 0%

profile of v1, /device:TPU:0, one launch (start us, length us, event | category | flops | bytes accessed | tf_op | source)
XLA Modules:
  0.0 639.4 jit_solution(18236620615264776908)
XLA Ops:
  25.8 11.9 %gather_fusion.3 = bf16[1280,2048]{1,0:T(8,128)(2,1)} fusion(bf16[129,2048]{1,0:T(8,128)(2,1)} %concatenate.14, s32[2048]{0:T(1024)S(1)} %pad_clamp_fusion), kind=kCustom, calls=%fused_computation.3 | custom fusion | bytes 10490880 | tf_op jit(solution)/shard_map/gather | solution.py:56
  37.8 5.8 fusion
  43.5 7.3 %all-to-all-start.1 = ((bf16[16,80,2048]{2,1,0:T(8,128)(2,1)}), bf16[16,80,2048]{2,1,0:T(8,128)(2,1)}, u32[]{:S(2)}, u32[]{:S(2)}) async-start(bf16[16,80,2048]{2,1,0:T(8,128)(2,1)} %fusion), calls=%async_computation.1 | async-start | bytes 10485760 | tf_op jit(solution)/shard_map/all_to_all | solution.py:60
  52.7 11.9 %gather_fusion = bf16[1280,2048]{1,0:T(8,128)(2,1)} fusion(bf16[129,2048]{1,0:T(8,128)(2,1)} %concatenate.13, s32[2048]{0:T(1024)S(1)} %pad_clamp_fusion), kind=kCustom, calls=%fused_computation | custom fusion | bytes 10490880 | tf_op jit(solution)/shard_map/gather | solution.py:55
  64.7 101.9 %all-to-all-done.1 = bf16[16,80,2048]{2,1,0:T(8,128)(2,1)} async-done(((bf16[16,80,2048]{2,1,0:T(8,128)(2,1)}), bf16[16,80,2048]{2,1,0:T(8,128)(2,1)}, u32[]{:S(2)}, u32[]{:S(2)}) %all-to-all-start.1) | async-done | bytes 5242912 | tf_op jit(solution)/shard_map/all_to_all | solution.py:60
  166.6 4.7 all-to-all-start
  171.8 5.7 copy.48
  177.5 108.6 %all-to-all-done = bf16[16,80,2048]{2,1,0:T(8,128)(2,1)} async-done(((bf16[16,80,2048]{2,1,0:T(8,128)(2,1)}), bf16[16,80,2048]{2,1,0:T(8,128)(2,1)}, u32[]{:S(2)}, u32[]{:S(2)}) %all-to-all-start) | async-done | bytes 5242912 | tf_op jit(solution)/shard_map/all_to_all | solution.py:58
  296.7 4.9 multiply_convert_fusion
  304.7 5.3 convert_bitcast_fusion
  309.9 8.6 %pad_maximum_fusion = bf16[2048,2,1152]{0,2,1:T(8,128)(2,1)} fusion(bf16[2048,2,384]{0,2,1:T(8,128)(2,1)S(1)} %fusion.3, bf16[2048,2,768]{0,2,1:T(8,128)(2,1)S(1)} %convert_bitcast_fusion), kind=kLoop, calls=%fused_computation.10 | loop fusion | flops 18874368 | bytes 18874368 | tf_op jit(solution)/shard_map/concatenate | solution.py:106
  318.6 5.4 fusion.23
  324.0 5.5 add_convert_fusion
  329.5 11.4 %copy.51 = bf16[2,640,2048]{2,0,1:T(2,128)(2,1)} copy(bf16[2,640,2048]{2,1,0:T(8,128)(2,1)} %add_convert_fusion) | data formatting | bytes 10485760 | tf_op jit(solution)/shard_map/convert_element_type | solution.py:94
  340.9 5.0 all-to-all-start.2
  362.7 40.4 %collective-permute-done = bf16[2,80,2048]{2,1,0:T(8,128)(2,1)S(1)} collective-permute-done((bf16[2,80,2048]{2,1,0:T(8,128)(2,1)S(1)}, bf16[2,80,2048]{2,1,0:T(8,128)(2,1)S(1)}, u32[]{:S(2)}, u32[]{:S(2)}) %collective-permute-start) | collective-permute-done | bytes 655392 | tf_op jit(solution)/shard_map/ppermute | solution.py:71
  406.3 82.2 %collective-permute-done.1 = bf16[2,80,2048]{2,1,0:T(8,128)(2,1)S(1)} collective-permute-done((bf16[2,80,2048]{2,1,0:T(8,128)(2,1)S(1)}, bf16[2,80,2048]{2,1,0:T(8,128)(2,1)S(1)}, u32[]{:S(2)}, u32[]{:S(2)}) %collective-permute-start.1) | collective-permute-done | bytes 655392 | tf_op jit(solution)/shard_map/ppermute | solution.py:71
  493.3 9.2 %collective-permute-done.2 = bf16[2,80,2048]{2,1,0:T(8,128)(2,1)S(1)} collective-permute-done((bf16[2,80,2048]{2,1,0:T(8,128)(2,1)S(1)}, bf16[2,80,2048]{2,1,0:T(8,128)(2,1)S(1)}, u32[]{:S(2)}, u32[]{:S(2)}) %collective-permute-start.2) | collective-permute-done | bytes 655392 | tf_op jit(solution)/shard_map/ppermute | solution.py:71
  503.4 70.0 %collective-permute-done.3 = bf16[2,80,2048]{2,1,0:T(8,128)(2,1)S(1)} collective-permute-done((bf16[2,80,2048]{2,1,0:T(8,128)(2,1)S(1)}, bf16[2,80,2048]{2,1,0:T(8,128)(2,1)S(1)}, u32[]{:S(2)}, u32[]{:S(2)}) %collective-permute-start.3) | collective-permute-done | bytes 655392 | tf_op jit(solution)/shard_map/ppermute | solution.py:71
  577.1 5.7 gather_fusion.1
  582.7 12.0 %gather_fusion.2 = bf16[1024,2048]{1,0:T(8,128)(2,1)} fusion(bf16[1280,2048]{1,0:T(8,128)(2,1)} %bitcast.106, s32[1024]{0:T(1024)S(1)} %broadcast_clamp_fusion), kind=kCustom, calls=%fused_computation.2 | custom fusion | bytes 8392704 | tf_op jit(solution)/shard_map/gather | solution.py:80
  599.2 7.2 %copy.52 = bf16[2,8,80,2048]{3,2,0,1:T(8,128)(2,1)} copy(bf16[2,8,80,2048]{3,0,2,1:T(2,128)(2,1)} %bitcast.33) | data formatting | bytes 10485760 | tf_op jit(solution)/shard_map/all_to_all | solution.py:95
  606.4 12.2 %gather_fusion.4 = bf16[1024,2048]{1,0:T(8,128)(2,1)} fusion(bf16[1280,2048]{1,0:T(8,128)(2,1)} %bitcast.107, s32[1024]{0:T(1024)S(1)} %broadcast_clamp_fusion), kind=kCustom, calls=%fused_computation.4 | custom fusion | bytes 8392704 | tf_op jit(solution)/shard_map/gather | solution.py:98
  618.6 5.9 bitcast_reduce_fusion
  (86 shorter events, 76.1 us)
Async XLA Ops:
  7.2 289.5 %copy-start = (bf16[2,384,2048]{2,1,0:T(8,128)(2,1)S(1)}, bf16[2,384,2048]{2,1,0:T(8,128)(2,1)}, u32[]{:S(2)}) copy-start(bf16[2,384,2048]{2,1,0:T(8,128)(2,1)} %param.13) | copy-start | bytes 9437188
  43.5 123.1 %all-to-all-start.1 = ((bf16[16,80,2048]{2,1,0:T(8,128)(2,1)}), bf16[16,80,2048]{2,1,0:T(8,128)(2,1)}, u32[]{:S(2)}, u32[]{:S(2)}) async-start(bf16[16,80,2048]{2,1,0:T(8,128)(2,1)} %fusion), calls=%async_computation.1 | async-start | bytes 10485760 | tf_op jit(solution)/shard_map/all_to_all | solution.py:60
  166.6 119.6 %all-to-all-start = ((bf16[16,80,2048]{2,1,0:T(8,128)(2,1)}), bf16[16,80,2048]{2,1,0:T(8,128)(2,1)}, u32[]{:S(2)}, u32[]{:S(2)}) async-start(bf16[16,80,2048]{2,1,0:T(8,128)(2,1)} %bitcast.108), calls=%async_computation | async-start | bytes 10485760 | tf_op jit(solution)/shard_map/all_to_all | solution.py:58
  171.3 453.2 %reduce-scatter.2.cloned.1.call-start = ((), (), s32[]{:S(2)}) async-start(), calls=%async_computation.4 | async-start | bytes 11796480 | tf_op jit(solution)/shard_map/reduce_scatter | solution.py:105
  286.2 3.4 copy-start.2
  289.6 2.9 copy-start.1
  289.6 7.1 %slice-start = ((s8[5242880]{0:T(1024)(128)(4,1)}), s8[4194304]{0:T(1024)(128)(4,1)S(1)}, s32[]{:S(2)}) async-start(s8[5242880]{0:T(1024)(128)(4,1)} %bitcast.110), calls=%async_computation.5 | async-start | bytes 8388608
  292.5 4.1 slice-start.1
  301.6 3.0 copy-start.8
  301.6 3.0 copy-start.4
  301.6 3.0 copy-start.5
  318.6 5.4 copy-start.3
  318.6 5.4 copy-start.6
  340.9 5.0 copy-start.7
  340.9 258.3 %all-to-all-start.2 = ((bf16[2,640,2048]{2,0,1:T(2,128)(2,1)}), bf16[2,640,2048]{2,0,1:T(2,128)(2,1)}, u32[]{:S(2)}, u32[]{:S(2)}) async-start(bf16[2,640,2048]{2,0,1:T(2,128)(2,1)} %copy.51), calls=%async_computation.2 | async-start | bytes 10485760 | tf_op jit(solution)/shard_map/all_to_all | solution.py:95
  351.1 52.0 %collective-permute-start = (bf16[2,80,2048]{2,1,0:T(8,128)(2,1)S(1)}, bf16[2,80,2048]{2,1,0:T(8,128)(2,1)S(1)}, u32[]{:S(2)}, u32[]{:S(2)}) collective-permute-start(bf16[2,80,2048]{2,1,0:T(8,128)(2,1)S(1)} %get-tuple-element.26), channel_id=1, source_target_pairs={{0,4},{4,0},{8,12},{12,8},{16,20},{20,16},{24,28},{28,24},{1,5},{5... | collective-permute-start | bytes 1966088 | tf_op jit(solution)/shard_map/ppermute | solution.py:71
  353.2 223.0 %collective-permute-start.6 = (bf16[2,80,2048]{2,1,0:T(8,128)(2,1)S(1)}, bf16[2,80,2048]{2,1,0:T(8,128)(2,1)S(1)}, u32[]{:S(2)}, u32[]{:S(2)}) collective-permute-start(bf16[2,80,2048]{2,1,0:T(8,128)(2,1)S(1)} %get-tuple-element.20), channel_id=1, source_target_pairs={{0,28},{4,24},{8,20},{12,16},{16,12},{20,8},{24,4},{28,0},{1,29},{... | collective-permute-start | bytes 1966088 | tf_op jit(solution)/shard_map/ppermute | solution.py:71
  356.5 218.7 %collective-permute-start.5 = (bf16[2,80,2048]{2,1,0:T(8,128)(2,1)S(1)}, bf16[2,80,2048]{2,1,0:T(8,128)(2,1)S(1)}, u32[]{:S(2)}, u32[]{:S(2)}) collective-permute-start(bf16[2,80,2048]{2,1,0:T(8,128)(2,1)S(1)} %get-tuple-element.21), channel_id=1, source_target_pairs={{0,24},{4,28},{8,16},{12,20},{16,8},{20,12},{24,0},{28,4},{1,25},{... | collective-permute-start | bytes 1966088 | tf_op jit(solution)/shard_map/ppermute | solution.py:71
  356.6 217.7 %collective-permute-start.4 = (bf16[2,80,2048]{2,1,0:T(8,128)(2,1)S(1)}, bf16[2,80,2048]{2,1,0:T(8,128)(2,1)S(1)}, u32[]{:S(2)}, u32[]{:S(2)}) collective-permute-start(bf16[2,80,2048]{2,1,0:T(8,128)(2,1)S(1)} %get-tuple-element.22), channel_id=1, source_target_pairs={{0,20},{4,16},{8,28},{12,24},{16,4},{20,0},{24,12},{28,8},{1,21},{... | collective-permute-start | bytes 1966088 | tf_op jit(solution)/shard_map/ppermute | solution.py:71
  358.5 129.9 %collective-permute-start.1 = (bf16[2,80,2048]{2,1,0:T(8,128)(2,1)S(1)}, bf16[2,80,2048]{2,1,0:T(8,128)(2,1)S(1)}, u32[]{:S(2)}, u32[]{:S(2)}) collective-permute-start(bf16[2,80,2048]{2,1,0:T(8,128)(2,1)S(1)} %get-tuple-element.25), channel_id=1, source_target_pairs={{0,8},{4,12},{8,0},{12,4},{16,24},{20,28},{24,16},{28,20},{1,9},{5... | collective-permute-start | bytes 1966088 | tf_op jit(solution)/shard_map/ppermute | solution.py:71
  403.2 99.3 %collective-permute-start.2 = (bf16[2,80,2048]{2,1,0:T(8,128)(2,1)S(1)}, bf16[2,80,2048]{2,1,0:T(8,128)(2,1)S(1)}, u32[]{:S(2)}, u32[]{:S(2)}) collective-permute-start(bf16[2,80,2048]{2,1,0:T(8,128)(2,1)S(1)} %get-tuple-element.24), channel_id=1, source_target_pairs={{0,12},{4,8},{8,4},{12,0},{16,28},{20,24},{24,20},{28,16},{1,13},{... | collective-permute-start | bytes 1966088 | tf_op jit(solution)/shard_map/ppermute | solution.py:71
  488.5 84.9 %collective-permute-start.3 = (bf16[2,80,2048]{2,1,0:T(8,128)(2,1)S(1)}, bf16[2,80,2048]{2,1,0:T(8,128)(2,1)S(1)}, u32[]{:S(2)}, u32[]{:S(2)}) collective-permute-start(bf16[2,80,2048]{2,1,0:T(8,128)(2,1)S(1)} %get-tuple-element.23), channel_id=1, source_target_pairs={{0,16},{4,20},{8,24},{12,28},{16,0},{20,4},{24,8},{28,12},{1,17},{... | collective-permute-start | bytes 1966088 | tf_op jit(solution)/shard_map/ppermute | solution.py:71
Sparse Core Ops, SparseCore 0:
  318.7 76.7 reduce-scatter.1
